TPU v7x, 32 devices: a whole 2x2x4 slice. The times are simulated.
32 devices in a mesh: region: 4 (over y, x), block: 8 (over z, core).
Axes of the slice: x: 2, y: 2, z: 4, core: 2. Of those that a mesh axis runs over, the one named last changes fastest.
Arguments:
- obs: bfloat16 [512, 32, 128], P(('region', 'block')), may hold values from -6 to 6
- predict: bfloat16 [512, 2, 128, 128], P(('region', 'block')), may hold values from -0.375 to 0.375
- factor: bfloat16 [512, 128, 128], P(('region', 'block')), as said below
- tau: float32 [32], replicated, may hold values from 0.5 to 2
- nbr_dev: int32 [512, 1], P(('region', 'block')), may hold values from 0 to 7; in each aligned block of 16 rows (0 to 15, 16 to 31, ...) at most 4 rows name the same one
- nbr_slot: int32 [512, 2], P(('region', 'block')), may hold values from 0 to 15
- counts: int32 [32], P(('region', 'block')), may hold values from 8 to 16
Outputs:
- grad_obs: float32 [512, 32, 128], P(('region', 'block'))
- grad_tau: float32 [32], replicated
Inputs may be any that keep to these rules, and one draw needn't show every extreme that they name: `nbr_dev`: among the blocks of one device at most 4 name the same device. `nbr_slot`: column 0 is a slot on the in-region neighbour's device, column 1 a slot on the device of the previous region with the same index along block. `factor`: each block's matrix is the identity plus small entries.
All inputs are finite; a program needn't handle non-finite values.
Results may differ from a plain program's by a relative error of at most 0.0035.
Values may be sent and summed in bfloat16 or wider, within the bound.
A program may use at most 64 MiB of HBM per device.

v0:
```python
import jax
import jax.numpy as jnp
from jax import lax
from jax.sharding import PartitionSpec as P


def passed_along(value, axis, steps):
    count = lax.axis_size(axis)
    leading, last = (max(0, -steps), min(count, count - steps))
    return lax.ppermute(value, axis, [(source, source + steps) for source in range(leading, last)])


def shards(obs, predict, factor, tau, nbr_dev, nbr_slot, counts):
    nbd = obs.shape[0]
    chans = obs.shape[1]
    width = obs.shape[2]
    nblock = lax.axis_size("block")
    cap_size = max(2, 2 * nbd // nblock)
    total_slots = nblock * cap_size
    dest = nbr_dev[:, 0]
    slot_one = nbr_slot[:, 0]
    slot_two = nbr_slot[:, 1]
    onehot = (dest[:, None] == jnp.arange(nblock, dtype=jnp.int32)[None, :]).astype(jnp.int32)
    before = jnp.cumsum(onehot, axis=0) - onehot
    rank_in = jnp.sum(before * onehot, axis=1)
    flat = dest * cap_size + rank_in
    match = (flat[:, None] == jnp.arange(total_slots, dtype=jnp.int32)[None, :]).astype(jnp.int32)
    filled = jnp.sum(match, axis=0)
    req_flat = jnp.sum(match * slot_one[:, None], axis=0) + (1 - filled) * nbd
    request = req_flat.reshape(nblock, cap_size)
    region_all = lax.all_gather(obs, "block", axis=0, tiled=True)
    near = jnp.take(region_all, dest * nbd + slot_one, axis=0)
    previous = passed_along(obs, "region", 1)
    far = jnp.take(previous, slot_two, axis=0)
    p_zero = predict[:, 0]
    p_one = predict[:, 1]
    err = obs.astype(jnp.float32) - jnp.einsum(
        "bcj,bjk->bck", near, p_zero, preferred_element_type=jnp.float32
    )
    err = err - jnp.einsum("bcj,bjk->bck", far, p_one, preferred_element_type=jnp.float32)
    err = err.astype(jnp.bfloat16)
    white = jnp.einsum("bcj,bjk->bck", err, factor, preferred_element_type=jnp.float32)
    live = (jnp.arange(nbd, dtype=jnp.int32) < counts[0]).astype(jnp.float32)
    weighted = (live[:, None, None] * tau[None, :, None] * white).astype(jnp.bfloat16)
    adj = jnp.einsum("bck,bjk->bcj", weighted, factor, preferred_element_type=jnp.float32)
    adj16 = adj.astype(jnp.bfloat16)
    back_one = -jnp.einsum("bck,bjk->bcj", adj16, p_zero, preferred_element_type=jnp.float32)
    back_two = -jnp.einsum("bck,bjk->bcj", adj16, p_one, preferred_element_type=jnp.float32)
    placed = jnp.einsum(
        "bs,bcj->scj", match.astype(jnp.float32), back_one, precision=lax.Precision.HIGHEST
    )
    placed = placed.reshape(nblock, cap_size, chans, width)
    returned, owned_slots = (
        lax.all_to_all(placed, "block", split_axis=0, concat_axis=0, tiled=True),
        lax.all_to_all(request, "block", split_axis=0, concat_axis=0, tiled=True),
    )
    spread = (owned_slots.reshape(-1)[:, None] == jnp.arange(nbd, dtype=jnp.int32)[None, :]).astype(
        jnp.float32
    )
    add_one = jnp.einsum(
        "sb,scj->bcj",
        spread,
        returned.reshape(total_slots, chans, width),
        precision=lax.Precision.HIGHEST,
    )
    seam_hot = (slot_two[:, None] == jnp.arange(nbd, dtype=jnp.int32)[None, :]).astype(jnp.float32)
    seam_dense = jnp.einsum("bs,bcj->scj", seam_hot, back_two, precision=lax.Precision.HIGHEST)
    add_two = passed_along(seam_dense, "region", -1)
    grad_obs = adj + add_one + add_two
    squares = jnp.sum(live[:, None, None] * white * white, axis=(0, 2))
    live_count = jnp.sum(live)
    total_sq, total_live = lax.psum((squares, live_count), ("region", "block"))
    all_blocks = nbd * lax.axis_size("region") * nblock
    grad_tau = (0.5 * total_sq - 0.5 * width * total_live / tau) / (all_blocks * width)
    return (grad_obs, grad_tau)


def solution(mesh):
    in_specs = (
        P(("region", "block"), None, None),
        P(("region", "block"), None, None, None),
        P(("region", "block"), None, None),
        P(),
        P(("region", "block"), None),
        P(("region", "block"), None),
        P(("region", "block")),
    )
    out_specs = (P(("region", "block"), None, None), P())
    return jax.shard_map(shards, mesh=mesh, in_specs=in_specs, out_specs=out_specs, check_vma=False)
```

profile of v0, /device:TPU:0, one launch (start us, length us, event | category | flops | bytes accessed | tf_op | source)
XLA Modules:
  0.0 102.5 jit_solution(590737278167899570)
XLA Ops:
  7.2 0.7 all-gather.2.cloned.1.call-update
  8.1 4.8 %collective-permute-start = (bf16[16,32,128]{2,1,0:T(8,128)(2,1)S(1)}, bf16[16,32,128]{2,1,0:T(8,128)(2,1)S(1)}, u32[]{:S(2)}, u32[]{:S(2)}) collective-permute-start(bf16[16,32,128]{2,1,0:T(8,128)(2,1)S(1)} %copy-done.2), channel_id=1, source_target_pairs={{0,8},{8,16},{16,24},{1,9},{9,17},{17,25},{2,10},{10,18},{18,26},{... | collective-permute-start | bytes 393224 | tf_op jit(solution)/shard_map/ppermute | solution.py:10
  13.0 0.7 fusion.33
  13.8 0.8 select_reduce_fusion.1
  14.6 0.8 slice_bitcast_fusion.1
  15.5 0.7 add.50
  16.1 4.9 %all-to-all-start = ((s32[8,1,4]{2,1,0:T(1,128)}), s32[8,1,4]{2,1,0:T(1,128)S(1)}, u32[]{:S(2)}, u32[]{:S(2)}) async-start(s32[8,1,4]{2,1,0:T(1,128)} %bitcast.11), calls=%async_computation | async-start | bytes 8192 | tf_op jit(solution)/shard_map/all_to_all | solution.py:55
  21.7 0.8 and_bitcast_fusion.1
  22.4 0.7 broadcast_multiply_fusion
  23.2 0.6 gather_fusion.1
  23.8 10.7 %all-gather.2.cloned.1.call-done = bf16[128,32,128]{2,1,0:T(8,128)(2,1)} async-done(((bf16[16,32,128]{2,1,0:T(8,128)(2,1)}), bf16[128,32,128]{2,1,0:T(8,128)(2,1)}) %all-gather.2.cloned.1.call-update) | async-done | bytes 1048592 | tf_op jit(solution)/shard_map/all_gather | solution.py:31
  34.5 1.8 %gather_fusion = bf16[16,32,128]{2,1,0:T(8,128)(2,1)S(1)} fusion(bf16[128,32,128]{2,1,0:T(8,128)(2,1)} %all-gather.2.cloned.1.call-done, s32[1024]{0:T(1024)S(1)} %pad_clamp_fusion.1), kind=kCustom, calls=%fused_computation | custom fusion | bytes 262208 | tf_op jit(solution)/shard_map/jit(_take)/gather | solution.py:32
  36.3 1.4 %convolution_subtract_fusion.1 = f32[16,32,128]{2,1,0:T(8,128)S(1)} fusion(bf16[16,2,128,128]{3,2,1,0:T(8,128)(2,1)} %param.8, bf16[16,32,128]{2,1,0:T(8,128)(2,1)S(1)} %copy-done.2, bf16[16,32,128]{2,1,0:T(8,128)(2,1)S(1)} %gather_fusion, pred[16]{0:T(512)(128)(4,1)S(1)} %get-tuple-element.6), kind=kOutput, calls=%fused_computation.5 | convolution fusion | flops 16973824 | bytes 1048592 | tf_op jit(solution)/shard_map/bcj,bjk->bck/dot_general | solution.py:37
  37.7 0.6 fusion.12
  39.0 0.7 fusion.16
  39.8 0.9 copy.17
  40.7 3.5 %all-to-all-start.1 = ((f32[8,4,32,128]{3,1,2,0:T(4,128)}), f32[8,4,32,128]{3,1,2,0:T(4,128)S(1)}, u32[]{:S(2)}, u32[]{:S(2)}) async-start(f32[8,4,32,128]{3,1,2,0:T(4,128)} %copy.17), calls=%async_computation.1 | async-start | bytes 1048576 | tf_op jit(solution)/shard_map/all_to_all | solution.py:54
  44.2 0.6 fusion.47
  45.3 0.7 reduce.3
  46.9 1.3 %collective-permute-start.1 = (f32[16,32,128]{2,1,0:T(8,128)S(1)}, f32[16,32,128]{2,1,0:T(8,128)S(1)}, u32[]{:S(2)}, u32[]{:S(2)}) collective-permute-start(f32[16,32,128]{2,1,0:T(8,128)S(1)} %copy.21), channel_id=1, source_target_pairs={{8,0},{16,8},{24,16},{9,1},{17,9},{25,17},{10,2},{18,10},{26,18},{... | collective-permute-start | bytes 786440 | tf_op jit(solution)/shard_map/ppermute | solution.py:10
  48.2 44.3 %all-reduce = (f32[32]{0:T(128)S(1)}, f32[]{:T(128)}) all-reduce(f32[32]{0:T(128)S(1)} %get-tuple-element.12, f32[]{:T(128)} %fusion.47), channel_id=1, replica_groups=mesh['region'=4,'block'=8] {'region','block'}, use_global_device_ids=true, to_apply=%region_5.6 | all-reduce | flops 33 | bytes 264 | tf_op jit(solution)/shard_map/psum | solution.py:72
  93.2 0.6 copy-done.3
  93.8 0.5 fusion.43
  94.8 0.9 fusion.15
  (27 shorter events, 3.1 us)
Async XLA Ops:
  7.2 30.5 %copy-start = (bf16[16,128,128]{2,1,0:T(8,128)(2,1)S(1)}, bf16[16,128,128]{2,1,0:T(8,128)(2,1)}, u32[]{:S(2)}) copy-start(bf16[16,128,128]{2,1,0:T(8,128)(2,1)} %param.9) | copy-start | bytes 1572868
  7.2 1.0 copy-start.2
  7.2 30.5 %copy-start.1 = (bf16[16,2,128,128]{3,2,1,0:T(8,128)(2,1)S(1)}, bf16[16,2,128,128]{3,2,1,0:T(8,128)(2,1)}, u32[]{:S(2)}) copy-start(bf16[16,2,128,128]{3,2,1,0:T(8,128)(2,1)} %param.8) | copy-start | bytes 3145732
  7.2 27.3 %all-gather.2.cloned.1.call-start = ((), (), s32[]{:S(2)}) async-start(), calls=%async_computation.2 | async-start | bytes 1179648 | tf_op jit(solution)/shard_map/all_gather | solution.py:31
  8.1 15.0 %collective-permute-start = (bf16[16,32,128]{2,1,0:T(8,128)(2,1)S(1)}, bf16[16,32,128]{2,1,0:T(8,128)(2,1)S(1)}, u32[]{:S(2)}, u32[]{:S(2)}) collective-permute-start(bf16[16,32,128]{2,1,0:T(8,128)(2,1)S(1)} %copy-done.2), channel_id=1, source_target_pairs={{0,8},{8,16},{16,24},{1,9},{9,17},{17,25},{2,10},{10,18},{18,26},{... | collective-permute-start | bytes 393224 | tf_op jit(solution)/shard_map/ppermute | solution.py:10
  16.1 24.5 %all-to-all-start = ((s32[8,1,4]{2,1,0:T(1,128)}), s32[8,1,4]{2,1,0:T(1,128)S(1)}, u32[]{:S(2)}, u32[]{:S(2)}) async-start(s32[8,1,4]{2,1,0:T(1,128)} %bitcast.11), calls=%async_computation | async-start | bytes 8192 | tf_op jit(solution)/shard_map/all_to_all | solution.py:55
  40.7 53.7 %all-to-all-start.1 = ((f32[8,4,32,128]{3,1,2,0:T(4,128)}), f32[8,4,32,128]{3,1,2,0:T(4,128)S(1)}, u32[]{:S(2)}, u32[]{:S(2)}) async-start(f32[8,4,32,128]{3,1,2,0:T(4,128)} %copy.17), calls=%async_computation.1 | async-start | bytes 1048576 | tf_op jit(solution)/shard_map/all_to_all | solution.py:54
  46.9 47.9 %collective-permute-start.1 = (f32[16,32,128]{2,1,0:T(8,128)S(1)}, f32[16,32,128]{2,1,0:T(8,128)S(1)}, u32[]{:S(2)}, u32[]{:S(2)}) collective-permute-start(f32[16,32,128]{2,1,0:T(8,128)S(1)} %copy.21), channel_id=1, source_target_pairs={{8,0},{16,8},{24,16},{9,1},{17,9},{25,17},{10,2},{18,10},{26,18},{... | collective-permute-start | bytes 786440 | tf_op jit(solution)/shard_map/ppermute | solution.py:10
  93.1 0.7 copy-start.3
Sparse Core Ops, SparseCore 0:
  9.6 24.7 all-gather.1
where the time goes:
time: 103 us
  blocking collectives  44.3 us (43%)
  between operations  15.5 us (15%)
  starting transfers between devices  14.5 us (14%)
  waiting for transfers between devices  11.4 us (11%)
  other arithmetic  6.61 us (6%)
  local copies, waits for them, and re-layouts  5.62 us (5%)
  matrix products  4.57 us (4%)
    psum x1, blocking collectives, shards(): total_sq, total_live = lax.psum((squares, live_count), ('region', 'block'))  44.3 us
    all_gather x1, waiting for transfers between devices, shards(): region_all = lax.all_gather(obs, 'block', axis=0, tiled=True)  10.7 us
    ppermute x2, starting transfers between devices, passed_along(): lax.ppermute(value, axis, [(source, source + steps) for source in range(l...  6.13 us
    all_to_all x1, starting transfers between devices, shards(): lax.all_to_all(request, 'block', split_axis=0, concat_axis=0, tiled=True)  4.88 us
    all_to_all x1, starting transfers between devices, shards(): lax.all_to_all(placed, 'block', split_axis=0, concat_axis=0, tiled=True)  3.49 us
  transfers between devices with their start and end apart: 5, of which 1 were waited for; matrix products, arithmetic and copies ran while one was open for 15% of the time, Pallas kernels for 0%

commit v1 on v0

--- a/solution.py
+++ b/solution.py
@@ -69,7 +69,7 @@
     grad_obs = adj + add_one + add_two
     squares = jnp.sum(live[:, None, None] * white * white, axis=(0, 2))
     live_count = jnp.sum(live)
-    total_sq, total_live = lax.psum((squares, live_count), ("region", "block"))
+    total_sq, total_live = lax.psum(lax.psum((squares, live_count), "block"), "region")
     all_blocks = nbd * lax.axis_size("region") * nblock
     grad_tau = (0.5 * total_sq - 0.5 * width * total_live / tau) / (all_blocks * width)
     return (grad_obs, grad_tau)

time: 103 us -> 87.9 us (0.85)
  blocking collectives: 44.3 us -> 29.2 us
    psum x1 -> x2, blocking collectives: 44.3 us -> 29.2 us  [the longest x1 18 us: shards(): lax.psum((squares, live_count), 'block')]
  transfers between devices with their start and end apart: 5 -> 5, of which waited for: 1 -> 1; matrix products, arithmetic and copies ran while one was open for 15% -> 17% of each run, Pallas kernels for 0% -> 0%
where the time goes in v1:
time: 87.9 us; the launch traced here: 87.4 us
  blocking collectives  29.2 us (33%)
  between operations  15.5 us (18%)
  starting transfers between devices  14.5 us (16%)
  waiting for transfers between devices  11.4 us (13%)
  other arithmetic  6.61 us (8%)
  local copies, waits for them, and re-layouts  5.62 us (6%)
  matrix products  4.57 us (5%)
    psum x1, blocking collectives, shards(): lax.psum((squares, live_count), 'block')  18 us
    psum x1, blocking collectives, shards(): lax.psum(lax.psum((squares, live_count), 'block'), 'region')  11.2 us
    all_gather x1, waiting for transfers between devices, shards(): region_all = lax.all_gather(obs, 'block', axis=0, tiled=True)  10.7 us
    ppermute x2, starting transfers between devices, passed_along(): lax.ppermute(value, axis, [(source, source + steps) for source in range(l...  6.13 us
    all_to_all x1, starting transfers between devices, shards(): lax.all_to_all(request, 'block', split_axis=0, concat_axis=0, tiled=True)  4.88 us
    all_to_all x1, starting transfers between devices, shards(): lax.all_to_all(placed, 'block', split_axis=0, concat_axis=0, tiled=True)  3.49 us
    gather x1, local copies, waits for them, and re-layouts, shards(): near = jnp.take(region_all, dest * nbd + slot_one, axis=0)  1.8 us
  transfers between devices with their start and end apart: 5, of which 1 were waited for; matrix products, arithmetic and copies ran while one was open for 17% of the time, Pallas kernels for 0%

profile of v1, /device:TPU:0, one launch (start us, length us, event | category | flops | bytes accessed | tf_op | source)
XLA Modules:
  0.0 87.4 jit_solution(10569275526177013040)
XLA Ops:
  7.2 0.7 all-gather.2.cloned.1.call-update
  8.1 4.8 %collective-permute-start = (bf16[16,32,128]{2,1,0:T(8,128)(2,1)S(1)}, bf16[16,32,128]{2,1,0:T(8,128)(2,1)S(1)}, u32[]{:S(2)}, u32[]{:S(2)}) collective-permute-start(bf16[16,32,128]{2,1,0:T(8,128)(2,1)S(1)} %copy-done.2), channel_id=1, source_target_pairs={{0,8},{8,16},{16,24},{1,9},{9,17},{17,25},{2,10},{10,18},{18,26},{... | collective-permute-start | bytes 393224 | tf_op jit(solution)/shard_map/ppermute | solution.py:10
  13.0 0.7 fusion.33
  13.8 0.8 select_reduce_fusion.1
  14.6 0.8 slice_bitcast_fusion.1
  15.5 0.7 add.54
  16.1 4.9 %all-to-all-start = ((s32[8,1,4]{2,1,0:T(1,128)}), s32[8,1,4]{2,1,0:T(1,128)S(1)}, u32[]{:S(2)}, u32[]{:S(2)}) async-start(s32[8,1,4]{2,1,0:T(1,128)} %bitcast.11), calls=%async_computation | async-start | bytes 8192 | tf_op jit(solution)/shard_map/all_to_all | solution.py:55
  21.7 0.8 and_bitcast_fusion.1
  22.4 0.7 broadcast_multiply_fusion
  23.2 0.6 gather_fusion.1
  23.8 10.7 %all-gather.2.cloned.1.call-done = bf16[128,32,128]{2,1,0:T(8,128)(2,1)} async-done(((bf16[16,32,128]{2,1,0:T(8,128)(2,1)}), bf16[128,32,128]{2,1,0:T(8,128)(2,1)}) %all-gather.2.cloned.1.call-update) | async-done | bytes 1048592 | tf_op jit(solution)/shard_map/all_gather | solution.py:31
  34.5 1.8 %gather_fusion = bf16[16,32,128]{2,1,0:T(8,128)(2,1)S(1)} fusion(bf16[128,32,128]{2,1,0:T(8,128)(2,1)} %all-gather.2.cloned.1.call-done, s32[1024]{0:T(1024)S(1)} %pad_clamp_fusion.1), kind=kCustom, calls=%fused_computation | custom fusion | bytes 262208 | tf_op jit(solution)/shard_map/jit(_take)/gather | solution.py:32
  36.3 1.4 %convolution_subtract_fusion.1 = f32[16,32,128]{2,1,0:T(8,128)S(1)} fusion(bf16[16,2,128,128]{3,2,1,0:T(8,128)(2,1)} %param.8, bf16[16,32,128]{2,1,0:T(8,128)(2,1)S(1)} %copy-done.2, bf16[16,32,128]{2,1,0:T(8,128)(2,1)S(1)} %gather_fusion, pred[16]{0:T(512)(128)(4,1)S(1)} %get-tuple-element.8), kind=kOutput, calls=%fused_computation.5 | convolution fusion | flops 16973824 | bytes 1048592 | tf_op jit(solution)/shard_map/bcj,bjk->bck/dot_general | solution.py:37
  37.7 0.6 fusion.12
  39.0 0.7 fusion.16
  39.8 0.9 %copy.17 = f32[8,4,32,128]{3,1,2,0:T(4,128)} copy(f32[8,4,32,128]{3,1,0,2:T(4,128)S(1)} %bitcast.53) | data formatting | bytes 1048576 | tf_op jit(solution)/shard_map/reshape | solution.py:52
  40.7 3.5 %all-to-all-start.1 = ((f32[8,4,32,128]{3,1,2,0:T(4,128)}), f32[8,4,32,128]{3,1,2,0:T(4,128)S(1)}, u32[]{:S(2)}, u32[]{:S(2)}) async-start(f32[8,4,32,128]{3,1,2,0:T(4,128)} %copy.17), calls=%async_computation.1 | async-start | bytes 1048576 | tf_op jit(solution)/shard_map/all_to_all | solution.py:54
  44.2 0.6 fusion.47
  45.3 0.7 reduce.3
  46.9 1.3 %collective-permute-start.1 = (f32[16,32,128]{2,1,0:T(8,128)S(1)}, f32[16,32,128]{2,1,0:T(8,128)S(1)}, u32[]{:S(2)}, u32[]{:S(2)}) collective-permute-start(f32[16,32,128]{2,1,0:T(8,128)S(1)} %copy.21), channel_id=1, source_target_pairs={{8,0},{16,8},{24,16},{9,1},{17,9},{25,17},{10,2},{18,10},{26,18},{... | collective-permute-start | bytes 786440 | tf_op jit(solution)/shard_map/ppermute | solution.py:10
  48.2 18.0 %all-reduce = (f32[32]{0:T(128)S(1)}, f32[]{:T(128)}) all-reduce(f32[32]{0:T(128)S(1)} %get-tuple-element.14, f32[]{:T(128)} %fusion.47), channel_id=1, replica_groups=mesh['region'=4,'block'=8] {'block'}, use_global_device_ids=true, to_apply=%region_5.6 | all-reduce | flops 33 | bytes 264 | tf_op jit(solution)/shard_map/psum | solution.py:72
  66.2 11.2 %all-reduce.1 = (f32[32]{0:T(128)S(1)}, f32[]{:T(128)}) all-reduce(f32[32]{0:T(128)S(1)} %get-tuple-element.4, f32[]{:T(128)} %get-tuple-element.5), channel_id=1, replica_groups=mesh['region'=4,'block'=8] {'region'}, use_global_device_ids=true, to_apply=%region_6.7 | all-reduce | flops 33 | bytes 264 | tf_op jit(solution)/shard_map/psum | solution.py:72
  78.1 0.6 copy-done.3
  79.7 0.9 fusion.15
  (28 shorter events, 3.7 us)
Async XLA Ops:
  7.2 30.5 %copy-start = (bf16[16,128,128]{2,1,0:T(8,128)(2,1)S(1)}, bf16[16,128,128]{2,1,0:T(8,128)(2,1)}, u32[]{:S(2)}) copy-start(bf16[16,128,128]{2,1,0:T(8,128)(2,1)} %param.9) | copy-start | bytes 1572868
  7.2 1.0 %copy-start.2 = (bf16[16,32,128]{2,1,0:T(8,128)(2,1)S(1)}, bf16[16,32,128]{2,1,0:T(8,128)(2,1)}, u32[]{:S(2)}) copy-start(bf16[16,32,128]{2,1,0:T(8,128)(2,1)} %param.7) | copy-start | bytes 393220
  7.2 30.5 %copy-start.1 = (bf16[16,2,128,128]{3,2,1,0:T(8,128)(2,1)S(1)}, bf16[16,2,128,128]{3,2,1,0:T(8,128)(2,1)}, u32[]{:S(2)}) copy-start(bf16[16,2,128,128]{3,2,1,0:T(8,128)(2,1)} %param.8) | copy-start | bytes 3145732
  7.2 27.3 %all-gather.2.cloned.1.call-start = ((), (), s32[]{:S(2)}) async-start(), calls=%async_computation.2 | async-start | bytes 1179648 | tf_op jit(solution)/shard_map/all_gather | solution.py:31
  8.1 15.0 %collective-permute-start = (bf16[16,32,128]{2,1,0:T(8,128)(2,1)S(1)}, bf16[16,32,128]{2,1,0:T(8,128)(2,1)S(1)}, u32[]{:S(2)}, u32[]{:S(2)}) collective-permute-start(bf16[16,32,128]{2,1,0:T(8,128)(2,1)S(1)} %copy-done.2), channel_id=1, source_target_pairs={{0,8},{8,16},{16,24},{1,9},{9,17},{17,25},{2,10},{10,18},{18,26},{... | collective-permute-start | bytes 393224 | tf_op jit(solution)/shard_map/ppermute | solution.py:10
  16.1 24.5 %all-to-all-start = ((s32[8,1,4]{2,1,0:T(1,128)}), s32[8,1,4]{2,1,0:T(1,128)S(1)}, u32[]{:S(2)}, u32[]{:S(2)}) async-start(s32[8,1,4]{2,1,0:T(1,128)} %bitcast.11), calls=%async_computation | async-start | bytes 8192 | tf_op jit(solution)/shard_map/all_to_all | solution.py:55
  40.7 38.6 %all-to-all-start.1 = ((f32[8,4,32,128]{3,1,2,0:T(4,128)}), f32[8,4,32,128]{3,1,2,0:T(4,128)S(1)}, u32[]{:S(2)}, u32[]{:S(2)}) async-start(f32[8,4,32,128]{3,1,2,0:T(4,128)} %copy.17), calls=%async_computation.1 | async-start | bytes 1048576 | tf_op jit(solution)/shard_map/all_to_all | solution.py:54
  46.9 32.8 %collective-permute-start.1 = (f32[16,32,128]{2,1,0:T(8,128)S(1)}, f32[16,32,128]{2,1,0:T(8,128)S(1)}, u32[]{:S(2)}, u32[]{:S(2)}) collective-permute-start(f32[16,32,128]{2,1,0:T(8,128)S(1)} %copy.21), channel_id=1, source_target_pairs={{8,0},{16,8},{24,16},{9,1},{17,9},{25,17},{10,2},{18,10},{26,18},{... | collective-permute-start | bytes 786440 | tf_op jit(solution)/shard_map/ppermute | solution.py:10
  78.1 0.7 copy-start.3
Sparse Core Ops, SparseCore 0:
  9.6 24.7 all-gather.1
